TPU v7x, 32 devices: a whole 2x2x4 slice. The times are simulated.
32 devices in a mesh: dp: 8 (over z, x), tensor: 4 (over y, core).
Axes of the slice: x: 2, y: 2, z: 4, core: 2. Of those that a mesh axis runs over, the one named last changes fastest.
Arguments:
- features: bfloat16 [32768, 768], P(('dp', 'tensor')), may hold values from -6 to 6
- first_gain: bfloat16 [768], replicated, may hold values from 0.5 to 1.5
- first_shift: bfloat16 [768], replicated, may hold values from -2 to 2
- qkv_weight: bfloat16 [768, 3, 768], P('dp', None, 'tensor'), may hold values from -0.21875 to 0.21875
- qv_bias: bfloat16 [2, 768], P(None, 'tensor'), may hold values from -1.1953125 to 1.1953125
- rel_height: bfloat16 [27, 64], replicated, may hold values from -0.59765625 to 0.59765625
- rel_width: bfloat16 [27, 64], replicated, may hold values from -0.59765625 to 0.59765625
- output_weight: bfloat16 [768, 768], P('dp', 'tensor'), may hold values from -1.25 to 1.25
- output_bias: bfloat16 [768], replicated, may hold values from -2 to 2
- second_gain: bfloat16 [768], replicated, may hold values from 0.5 to 1.5
- second_shift: bfloat16 [768], replicated, may hold values from -2 to 2
- up_weight: bfloat16 [768, 3072], P('dp', 'tensor'), may hold values from -0.21875 to 0.21875
- up_bias: bfloat16 [3072], P('tensor'), may hold values from -2 to 2
- down_weight: bfloat16 [768, 3072], P('dp', 'tensor'), may hold values from -0.109375 to 0.109375
- down_bias: bfloat16 [768], replicated, may hold values from -2 to 2
- cotangent: bfloat16 [32768, 768], P(('dp', 'tensor')), may hold values from -6 to 6
Outputs:
- output: bfloat16 [32768, 768], P(('dp', 'tensor'))
- grad_features: bfloat16 [32768, 768], P(('dp', 'tensor'))
- grad_first_gain: float32 [768], replicated
- grad_first_shift: float32 [768], replicated
- grad_qkv_weight: float32 [768, 3, 768], P('dp', None, 'tensor')
- grad_qv_bias: float32 [2, 768], P(None, 'tensor')
- grad_rel_height: float32 [27, 64], replicated
- grad_rel_width: float32 [27, 64], replicated
- grad_output_weight: float32 [768, 768], P('dp', 'tensor')
- grad_output_bias: float32 [768], replicated
- grad_second_gain: float32 [768], replicated
- grad_second_shift: float32 [768], replicated
- grad_up_weight: float32 [768, 3072], P('dp', 'tensor')
- grad_up_bias: float32 [3072], P('tensor')
- grad_down_weight: float32 [768, 3072], P('dp', 'tensor')
- grad_down_bias: float32 [768], replicated
All inputs are finite; a program needn't handle non-finite values.
Results may differ from a plain program's by a relative error of at most 0.015.
Values may be sent and summed in bfloat16 or wider, within the bound.
No kernel may reach another device: no remote copies, remote signals or barrier semaphores. Data moves between devices by JAX's collectives and lax.ppermute only.
A program may use at most 192 MiB of HBM per device.

v0:
```python
from functools import partial
import math
import jax
import jax.numpy as jnp
from jax import lax
from jax.sharding import PartitionSpec as P

D = 768
HD = 64
GRID = 64
WIN = 14
SIDE = 5
EPSILON = 1e-06
HIGH = lax.Precision.HIGHEST


def norm_parts(value):
    mean_value = jnp.mean(value, -1, keepdims=True)
    centered = value - mean_value
    inverse_deviation = lax.rsqrt(jnp.mean(centered * centered, -1, keepdims=True) + EPSILON)
    return (centered * inverse_deviation, inverse_deviation)


def norm_backward(upstream_gradient, normalized_input, inverse_deviation, gain_factor):
    scaled_input = upstream_gradient * gain_factor
    inner_product = (
        scaled_input
        - jnp.mean(scaled_input, -1, keepdims=True)
        - normalized_input * jnp.mean(scaled_input * normalized_input, -1, keepdims=True)
    )
    return (
        inverse_deviation * inner_product,
        jnp.sum(upstream_gradient * normalized_input, 0),
        jnp.sum(upstream_gradient, 0),
    )


def to_windows(flat, images):
    width = flat.shape[-1]
    extra = SIDE * WIN - GRID
    grid = jnp.pad(
        flat.reshape(images, GRID, GRID, width), ((0, 0), (0, extra), (0, extra), (0, 0))
    )
    grid = grid.reshape(images, SIDE, WIN, SIDE, WIN, width).transpose(0, 1, 3, 2, 4, 5)
    return grid.reshape(images * SIDE * SIDE, WIN * WIN, width)


def from_windows(windows, images):
    width = windows.shape[-1]
    grid = windows.reshape(images, SIDE, SIDE, WIN, WIN, width).transpose(0, 1, 3, 2, 4, 5)
    grid = grid.reshape(images, SIDE * WIN, SIDE * WIN, width)
    return grid[:, :GRID, :GRID].reshape(images * GRID * GRID, width)


def offset_table():
    offsets = jnp.arange(WIN)[:, None] - jnp.arange(WIN)[None, :] + WIN - 1
    return (offsets[:, :, None] == jnp.arange(2 * WIN - 1)[None, None, :]).astype(jnp.float32)


def spread_table():
    places = jnp.arange(WIN * WIN)
    marks = jnp.arange(WIN)[:, None]
    row_part = places[None, :] // WIN == marks
    col_part = places[None, :] % WIN == marks
    return jnp.concatenate([row_part, col_part], 0).astype(jnp.float32)


def contract_first(left, right):
    return lax.dot_general(
        left, right, (((0,), (0,)), ((), ())), preferred_element_type=jnp.float32
    )


def contract_last(left, right):
    return lax.dot_general(
        left, right, (((1,), (1,)), ((), ())), preferred_element_type=jnp.float32
    )


def scores_of(query, keys, table_rows, table_cols, spread):
    blocks, heads = (query.shape[0], query.shape[2])
    scores = jnp.einsum(
        "nqhc,nkhc->nhqk", query, keys, preferred_element_type=jnp.float32
    ) * HD ** (-0.5)
    query_grid = query.reshape(blocks, WIN, WIN, heads, HD)
    along_rows = jnp.einsum(
        "nabhc,akc->nhabk", query_grid, table_rows, preferred_element_type=jnp.float32
    )
    along_cols = jnp.einsum(
        "nabhc,bkc->nhabk", query_grid, table_cols, preferred_element_type=jnp.float32
    )
    along = jnp.concatenate([along_rows, along_cols], -1).reshape(blocks, heads, WIN * WIN, 2 * WIN)
    return scores + jnp.einsum("nhqj,jk->nhqk", along, spread, precision=HIGH)


def attend(tables, block):
    scores = scores_of(block[:, :, 0], block[:, :, 1], tables[0], tables[1], tables[2])
    largest = jnp.max(scores, -1, keepdims=True)
    log_total = largest + jnp.log(jnp.sum(jnp.exp(scores - largest), -1, keepdims=True))
    probs = jnp.exp(scores - log_total).astype(jnp.bfloat16)
    attended = jnp.einsum(
        "nhqk,nkhc->nqhc", probs, block[:, :, 2], preferred_element_type=jnp.float32
    )
    return (attended.astype(jnp.bfloat16), log_total)


def attend_back(tables, carry, items):
    block, upstream_gradient, log_total = items
    query, keys, values = (block[:, :, 0], block[:, :, 1], block[:, :, 2])
    blocks, heads = (query.shape[0], query.shape[2])
    probs = jnp.exp(scores_of(query, keys, tables[0], tables[1], tables[2]) - log_total)
    grad_values = jnp.einsum(
        "nhqk,nqhc->nkhc",
        probs.astype(jnp.bfloat16),
        upstream_gradient,
        preferred_element_type=jnp.float32,
    )
    grad_probs = jnp.einsum(
        "nqhc,nkhc->nhqk", upstream_gradient, values, preferred_element_type=jnp.float32
    )
    grad_scores = (probs * (grad_probs - jnp.sum(probs * grad_probs, -1, keepdims=True))).astype(
        jnp.bfloat16
    )
    grad_query = jnp.einsum(
        "nhqk,nkhc->nqhc", grad_scores, keys, preferred_element_type=jnp.float32
    ) * HD ** (-0.5)
    grad_keys = jnp.einsum(
        "nhqk,nqhc->nkhc", grad_scores, query, preferred_element_type=jnp.float32
    ) * HD ** (-0.5)
    key_sums = jnp.einsum(
        "nhqk,jk->nhqj", grad_scores, tables[3], preferred_element_type=jnp.float32
    )
    key_sums = key_sums.reshape(blocks, heads, WIN, WIN, 2 * WIN)
    sum_rows = key_sums[..., :WIN]
    sum_cols = key_sums[..., WIN:]
    rows_float = tables[0].astype(jnp.float32)
    cols_float = tables[1].astype(jnp.float32)
    extra = jnp.einsum("nhabk,akc->nabhc", sum_rows, rows_float, precision=HIGH)
    extra = extra + jnp.einsum("nhabk,bkc->nabhc", sum_cols, cols_float, precision=HIGH)
    grad_query = grad_query + extra.reshape(blocks, WIN * WIN, heads, HD)
    query_float = query.astype(jnp.float32).reshape(blocks, WIN, WIN, heads, HD)
    table_grad_rows = carry[0] + jnp.einsum(
        "nhabk,nabhc->akc", sum_rows, query_float, precision=HIGH
    )
    table_grad_cols = carry[1] + jnp.einsum(
        "nhabk,nabhc->bkc", sum_cols, query_float, precision=HIGH
    )
    grads = jnp.stack([grad_query, grad_keys, grad_values], axis=2).astype(jnp.bfloat16)
    return ((table_grad_rows, table_grad_cols), grads)


def gelu_slope(upper):
    return 0.5 * (1.0 + lax.erf(upper / math.sqrt(2.0))) + upper * jnp.exp(
        -0.5 * upper * upper
    ) / math.sqrt(2.0 * math.pi)


def feed_rows(normed, up_full, up_shift, down_full):
    upper = jnp.dot(normed, up_full, preferred_element_type=jnp.float32) + up_shift
    active = jax.nn.gelu(upper, approximate=False).astype(jnp.bfloat16)
    return contract_last(active, down_full)


def feed_back_rows(normed, grads, up_full, up_shift, down_full, block):
    steps = normed.shape[0] // block
    hidden = up_full.shape[1]

    def step(carry, items):
        part_in, part_grad = items
        upper = jnp.dot(part_in, up_full, preferred_element_type=jnp.float32) + up_shift
        active = jax.nn.gelu(upper, approximate=False).astype(jnp.bfloat16)
        slope = jnp.dot(part_grad, down_full, preferred_element_type=jnp.float32)
        delta = (slope * gelu_slope(upper)).astype(jnp.bfloat16)
        grad_up = carry[0] + contract_first(part_in, delta)
        grad_down = carry[1] + contract_first(part_grad, active)
        grad_shift = carry[2] + jnp.sum(delta.astype(jnp.float32), 0)
        return ((grad_up, grad_down, grad_shift), delta)

    start_carry = (
        jnp.zeros((D, hidden), jnp.float32),
        jnp.zeros((D, hidden), jnp.float32),
        jnp.zeros((hidden,), jnp.float32),
    )
    carry, deltas = lax.scan(
        step, start_carry, (normed.reshape(steps, block, D), grads.reshape(steps, block, D))
    )
    return (deltas.reshape(steps * block, hidden), carry[0], carry[1], carry[2])


def body(
    features,
    first_gain,
    first_shift,
    qkv_weight,
    qv_bias,
    rel_height,
    rel_width,
    output_weight,
    output_bias,
    second_gain,
    second_shift,
    up_weight,
    up_bias,
    down_weight,
    down_bias,
    cotangent,
):
    qkv_full, output_full, up_full, down_full = (
        lax.all_gather(qkv_weight, "dp", axis=0, tiled=True),
        lax.all_gather(output_weight, "dp", axis=0, tiled=True),
        lax.all_gather(up_weight, "dp", axis=0, tiled=True),
        lax.all_gather(down_weight, "dp", axis=0, tiled=True),
    )
    local_width = qkv_weight.shape[2]
    heads_here = local_width // HD
    own_rows = features.shape[0]
    gain_one = first_gain.astype(jnp.float32)
    gain_two = second_gain.astype(jnp.float32)
    feature_float = features.astype(jnp.float32)
    hat_one, inverse_one = norm_parts(feature_float)
    normed_one = (hat_one * gain_one + first_shift.astype(jnp.float32)).astype(jnp.bfloat16)
    normed_all = lax.all_gather(normed_one, "tensor", axis=0, tiled=True)
    images = normed_all.shape[0] // (GRID * GRID)
    normed_windows = to_windows(normed_all, images)
    bias_float = qv_bias.astype(jnp.float32)
    bias_all = jnp.stack([bias_float[0], jnp.zeros_like(bias_float[0]), bias_float[1]]).reshape(
        3 * local_width
    )
    qkv_matrix = qkv_full.reshape(D, 3 * local_width)
    qkv = (
        jnp.dot(normed_windows.reshape(-1, D), qkv_matrix, preferred_element_type=jnp.float32)
        + bias_all
    )
    qkv = qkv.astype(jnp.bfloat16).reshape(images * SIDE, SIDE, WIN * WIN, 3, heads_here, HD)
    onehot = offset_table()
    onehot_low = onehot.astype(jnp.bfloat16)
    spread = spread_table()
    table_rows = jnp.einsum(
        "akr,rc->akc", onehot_low, rel_height, preferred_element_type=jnp.float32
    ).astype(jnp.bfloat16)
    table_cols = jnp.einsum(
        "akr,rc->akc", onehot_low, rel_width, preferred_element_type=jnp.float32
    ).astype(jnp.bfloat16)
    tables = (table_rows, table_cols, spread, spread.astype(jnp.bfloat16))
    attended, log_total = lax.map(partial(attend, tables), qkv)
    on_grid = from_windows(attended.reshape(images * SIDE * SIDE, WIN * WIN, local_width), images)
    branch = lax.psum_scatter(
        contract_last(on_grid, output_full), "tensor", scatter_dimension=0, tiled=True
    )
    branch = branch + output_bias.astype(jnp.float32)
    hidden_one = feature_float + branch
    hat_two, inverse_two = norm_parts(hidden_one)
    normed_two = (hat_two * gain_two + second_shift.astype(jnp.float32)).astype(jnp.bfloat16)
    up_shift = up_bias.astype(jnp.float32)
    normed_two_all = lax.all_gather(normed_two, "tensor", axis=0, tiled=True)
    feed = lax.psum_scatter(
        feed_rows(normed_two_all, up_full, up_shift, down_full).astype(jnp.bfloat16),
        "tensor",
        scatter_dimension=0,
        tiled=True,
    ).astype(jnp.float32)
    grads_all = lax.all_gather(cotangent, "tensor", axis=0, tiled=True)
    deltas, grad_up, grad_down, grad_up_shift = feed_back_rows(
        normed_two_all, grads_all, up_full, up_shift, down_full, own_rows
    )
    grad_normed_two = lax.psum_scatter(
        contract_last(deltas, up_full), "tensor", scatter_dimension=0, tiled=True
    )
    output = (hidden_one + feed + down_bias.astype(jnp.float32)).astype(jnp.bfloat16)
    grad_float = cotangent.astype(jnp.float32)
    grad_down_shift = jnp.sum(grad_float, 0)
    back_two, grad_gain_two, grad_shift_two = norm_backward(
        grad_normed_two, hat_two, inverse_two, gain_two
    )
    grad_hidden_one = grad_float + back_two
    grad_branch = grad_hidden_one.astype(jnp.bfloat16)
    grad_output_shift = jnp.sum(grad_branch.astype(jnp.float32), 0)
    grad_branch_all = lax.all_gather(grad_branch, "tensor", axis=0, tiled=True)
    grad_output = contract_first(grad_branch_all, on_grid)
    grad_on_grid = jnp.dot(grad_branch_all, output_full, preferred_element_type=jnp.float32).astype(
        jnp.bfloat16
    )
    grad_windows = to_windows(grad_on_grid, images).reshape(
        images * SIDE, SIDE, WIN * WIN, heads_here, HD
    )
    zero_table = jnp.zeros((WIN, WIN, HD), jnp.float32)
    table_grads, grad_qkv = lax.scan(
        partial(attend_back, tables), (zero_table, zero_table), (qkv, grad_windows, log_total)
    )
    grad_qkv = grad_qkv.reshape(images * SIDE * SIDE, WIN * WIN, 3 * local_width)
    shift_sums = jnp.sum(grad_qkv.astype(jnp.float32), (0, 1)).reshape(3, local_width)
    grad_qv_shift = jnp.stack([shift_sums[0], shift_sums[2]])
    grad_qkv_grid = from_windows(grad_qkv, images)
    grad_qkv_weight = contract_first(normed_all, grad_qkv_grid).reshape(D, 3, local_width)
    grad_normed_one = lax.psum_scatter(
        contract_last(grad_qkv_grid, qkv_matrix).astype(jnp.bfloat16),
        "tensor",
        scatter_dimension=0,
        tiled=True,
    ).astype(jnp.float32)
    grad_rel_rows = jnp.einsum("akr,akc->rc", onehot, table_grads[0], precision=HIGH)
    grad_rel_cols = jnp.einsum("akr,akc->rc", onehot, table_grads[1], precision=HIGH)
    back_one, grad_gain_one, grad_shift_one = norm_backward(
        grad_normed_one, hat_one, inverse_one, gain_one
    )
    grad_features = (grad_hidden_one + back_one).astype(jnp.bfloat16)
    grad_qkv_weight, grad_output, grad_up, grad_down = (
        lax.psum_scatter(grad_qkv_weight, "dp", scatter_dimension=0, tiled=True),
        lax.psum_scatter(grad_output, "dp", scatter_dimension=0, tiled=True),
        lax.psum_scatter(grad_up, "dp", scatter_dimension=0, tiled=True),
        lax.psum_scatter(grad_down, "dp", scatter_dimension=0, tiled=True),
    )
    (
        grad_gain_one,
        grad_shift_one,
        grad_gain_two,
        grad_shift_two,
        grad_output_shift,
        grad_down_shift,
        grad_rel_rows,
        grad_rel_cols,
    ) = lax.psum(
        (
            grad_gain_one,
            grad_shift_one,
            grad_gain_two,
            grad_shift_two,
            grad_output_shift,
            grad_down_shift,
            grad_rel_rows,
            grad_rel_cols,
        ),
        ("dp", "tensor"),
    )
    grad_qv_shift, grad_up_shift = lax.psum((grad_qv_shift, grad_up_shift), "dp")
    return (
        output,
        grad_features,
        grad_gain_one,
        grad_shift_one,
        grad_qkv_weight,
        grad_qv_shift,
        grad_rel_rows,
        grad_rel_cols,
        grad_output,
        grad_output_shift,
        grad_gain_two,
        grad_shift_two,
        grad_up,
        grad_up_shift,
        grad_down,
        grad_down_shift,
    )


def solution(mesh):
    placed = (
        P(("dp", "tensor"), None),
        P(),
        P(),
        P("dp", None, "tensor"),
        P(None, "tensor"),
        P(),
        P(),
        P("dp", "tensor"),
        P(),
        P(),
        P(),
        P("dp", "tensor"),
        P("tensor"),
        P("dp", "tensor"),
        P(),
        P(("dp", "tensor"), None),
    )
    return jax.shard_map(
        body,
        mesh=mesh,
        in_specs=placed,
        out_specs=(
            P(("dp", "tensor"), None),
            P(("dp", "tensor"), None),
            P(),
            P(),
            P("dp", None, "tensor"),
            P(None, "tensor"),
            P(),
            P(),
            P("dp", "tensor"),
            P(),
            P(),
            P(),
            P("dp", "tensor"),
            P("tensor"),
            P("dp", "tensor"),
            P(),
        ),
        check_vma=False,
    )
```

profile of v0, /device:TPU:0, one launch (start us, length us, event | category | flops | bytes accessed | tf_op | source)
XLA Modules:
  0.0 1442.1 jit_solution(18093629953301397693)
XLA Ops:
  14.9 38.8 %all_gather.25 = bf16[768,3,192]{2,1,0:T(4,128)(2,1)S(1)} all-gather(bf16[96,3,192]{2,1,0:T(4,128)(2,1)S(1)} %copy.162), channel_id=1, replica_groups=mesh['dp'=8,'tensor'=4] {'dp'}, dimensions={0}, use_global_device_ids=true | all-gather | bytes 995328 | tf_op jit(solution)/shard_map/all_gather | solution.py:209
  55.4 33.1 %all_gather.26 = bf16[768,192]{1,0:T(8,128)(2,1)} all-gather(bf16[96,192]{1,0:T(8,128)(2,1)S(1)} %copy-done.48), channel_id=1, replica_groups=mesh['dp'=8,'tensor'=4] {'dp'}, dimensions={0}, use_global_device_ids=true | all-gather | bytes 331776 | tf_op jit(solution)/shard_map/all_gather | solution.py:210
  89.0 6.5 pad.8
  95.5 11.5 reshape.269
  107.0 7.8 copy.161
  114.8 12.2 reshape_reshape.12
  127.0 9.8 add_convert_fusion
  136.8 17.7 %reshape.271 = bf16[5,5,196,3,3,64]{2,1,0,5,4,3:T(8,128)(2,1)} reshape(bf16[4900,576]{0,1:T(8,128)(2,1)} %add_convert_fusion) | data formatting | bytes 11289600 | tf_op jit(solution)/shard_map/reshape | solution.py:234
  154.5 9.7 copy.164
  164.1 62.1 %while.44 = (s32[]{:T(128)}, bf16[5,5,196,3,64]{2,4,3,1,0:T(8,128)(2,1)}, f32[5,5,3,196,1]{3,2,1,4,0:T(4,128)}, bf16[5,5,196,3,3,64]{2,5,4,1,3,0:T(8,128)(2,1)},...) while((s32[]{:T(128)}, ...), condition=%wide.region_5.6_spmd, body=%wide.region_2.5_spmd.sunk | while | flops 355972256 | bytes 23991828 | solution.py:245
  226.2 8.9 copy.165
  235.1 9.3 reshape_reshape.13
  251.9 6.3 fusion.247
  260.1 96.8 %reduce-scatter.9.cloned.1.call-done = f32[1024,768]{1,0:T(8,128)} async-done(((f32[4096,768]{1,0:T(8,128)}), f32[1024,768]{1,0:T(8,128)}) %reduce-scatter.9.cloned.1.call-update) | async-done | bytes 3145744 | tf_op jit(solution)/shard_map/reduce_scatter | solution.py:247
  363.5 26.8 %all-gather.15.cloned.1.call-done = bf16[4096,768]{1,0:T(8,128)(2,1)} async-done(((bf16[1024,768]{1,0:T(8,128)(2,1)}), bf16[4096,768]{1,0:T(8,128)(2,1)}) %all-gather.15.cloned.1.call-update) | async-done | bytes 6291472 | tf_op jit(solution)/shard_map/all_gather | solution.py:262
  390.2 48.4 %all-gather.9.cloned.1.call-done = bf16[4096,768]{1,0:T(8,128)(2,1)} async-done(((bf16[1024,768]{1,0:T(8,128)(2,1)}), bf16[4096,768]{1,0:T(8,128)(2,1)}) %all-gather.9.cloned.1.call-update) | async-done | bytes 6291472 | tf_op jit(solution)/shard_map/all_gather | solution.py:255
  438.7 101.8 %while.45 = (s32[]{:T(128)}, f32[768,768]{1,0:T(8,128)}, f32[768,768]{1,0:T(8,128)}, f32[768]{0:T(1024)S(1)}, bf16[4,1024,768]{2,1,0:T(8,128)(2,1)}, /*index=5*/...) while((s32[]{:T(128)}, f32[768,768]{1,0:T(8,128)}, ...), condition=%wide.region_12.13_spmd.clone, body=%wide.region_10.12_spmd.clone.sunk | while | flops 4896326144 | bytes 63722192 | solution.py:184
  442.1 5.3 convert_reduce_fusion.7
  453.3 10.3 select_add_fusion.7
  466.8 5.3 convert_reduce_fusion.7
  478.7 10.5 select_add_fusion.7
  492.5 5.3 convert_reduce_fusion.7
  504.3 10.5 select_add_fusion.7
  518.1 5.3 convert_reduce_fusion.7
  529.9 10.5 select_add_fusion.7
  540.4 10.1 fusion.248
  552.2 38.3 %convolution_convert_fusion.1 = bf16[4096,768]{1,0:T(8,128)(2,1)} fusion(bf16[768,768]{1,0:T(8,128)(2,1)S(1)} %copy-done.63, f32[768]{0:T(1024)S(1)} %get-tuple-element.757, bf16[4096,768]{1,0:T(8,128)(2,1)} %bitcast.323, bf16[768,768]{1,0:T(8,128)(2,1)S(1)} %copy-done.61), kind=kOutput, calls=%fused_computation.213 | convolution fusion | flops 9874440192 | bytes 14945280 | tf_op jit(solution)/shard_map/dot_general | solution.py:75
  591.2 58.4 %reduce-scatter.13.cloned.1.call-done = f32[1024,768]{1,0:T(8,128)} async-done(((f32[4096,768]{1,0:T(8,128)}), f32[1024,768]{1,0:T(8,128)}) %reduce-scatter.13.cloned.1.call-update) | async-done | bytes 3145744 | tf_op jit(solution)/shard_map/reduce_scatter | solution.py:266
  653.3 57.1 %reduce-scatter.11.cloned.1.call-done = bf16[1024,768]{1,0:T(8,128)(2,1)} async-done(((bf16[4096,768]{1,0:T(8,128)(2,1)}), bf16[1024,768]{1,0:T(8,128)(2,1)}) %reduce-scatter.11.cloned.1.call-update) | async-done | bytes 1572880 | tf_op jit(solution)/shard_map/reduce_scatter | solution.py:256
  710.5 6.1 convert_reduce_fusion.5
  716.6 46.5 %all-gather.17.cloned.1.call-done = bf16[4096,768]{1,0:T(8,128)(2,1)} async-done(((bf16[1024,768]{1,0:T(8,128)(2,1)}), bf16[4096,768]{1,0:T(8,128)(2,1)}) %all-gather.17.cloned.1.call-update) | async-done | bytes 6291472 | tf_op jit(solution)/shard_map/all_gather | solution.py:278
  777.9 5.3 reshape_reshape.14
  783.2 8.5 copy.170
  791.7 223.9 %while.46 = (s32[]{:T(128)}, f32[14,14,64]{2,1,0:T(8,128)S(1)}, f32[14,14,64]{2,1,0:T(8,128)S(1)}, bf16[5,5,196,3,3,64]{2,5,4,1,3,0:T(8,128)(2,1)}, bf16[5,5,196...) while((s32[]{:T(128)}, f32[14,14,64]{2,1,0:T(8,128)S(1)}, ...), condition=%wide.region_18.19_spmd.clone, body=%wide.region_16.18_spmd.clone.sunk | while | flops 741679872 | bytes 70086392 | solution.py:287
  1015.6 20.7 %copy.171 = bf16[5,5,196,3,3,64]{5,4,3,2,1,0:T(4,128)(2,1)} copy(bf16[5,5,196,3,3,64]{2,5,4,1,3,0:T(8,128)(2,1)} %get-tuple-element.171) | data formatting | bytes 11289600 | tf_op jit(solution)/shard_map/while | solution.py:287
  1036.3 26.7 %reshape_reshape.15 = bf16[1,5,5,14,14,576]{5,4,3,2,1,0:T(8,128)(2,1)} reshape(bf16[5,5,196,3,3,64]{5,4,3,2,1,0:T(4,128)(2,1)} %copy.171) | data formatting | bytes 11289600 | tf_op jit(solution)/shard_map/reshape;reshape | solution.py:50
  1063.0 6.5 copy.172
  1069.4 10.7 reshape.279
  1085.4 6.9 convolution_convert_fusion
  1093.6 8.0 copy.173
  1101.6 6.4 fusion.249
  1108.1 9.7 fusion.182
  1122.6 22.5 %all-reduce.3 = (f32[2,192]{1,0:T(2,128)}, f32[768]{0:T(1024)}) all-reduce(f32[2,192]{1,0:T(2,128)S(1)} %pad_maximum_fusion.3, f32[768]{0:T(1024)S(1)} %copy-done.32), channel_id=1, replica_groups=mesh['dp'=8,'tensor'=4] {'dp'}, use_global_device_ids=true, to_apply=%region_28.29 | all-reduce | flops 1152 | bytes 9216 | tf_op jit(solution)/shard_map/psum | solution.py:335
  1154.0 41.7 %all-reduce.2 = (f32[768]{0:T(1024)}, f32[768]{0:T(1024)}, f32[27,64]{1,0:T(8,128)}, f32[27,64]{1,0:T(8,128)}, f32[768]{0:T(1024)}, /*index=5*/f32[768]{0:T(1024)}, f32[768]{0:T(1024)}, f32[768]{0:T(1024)}) all-reduce(f32[768]{0:T(1024)S(1)} %get-tuple-element.320, ...), channel_id=1, replica_groups=mesh['dp'=8,'tensor'=4] {'dp','tensor'}, use_global_device_ids=true, to_apply=%region_23.24 | all-reduce | flops 8064 | bytes 64512 | tf_op jit(solution)/shard_map/psum | solution.py:322
  1199.4 25.2 %reduce-scatter.21.cloned.1.call-done = f32[96,768]{1,0:T(8,128)} async-done(((f32[768,768]{1,0:T(8,128)}), f32[96,768]{1,0:T(8,128)}) %reduce-scatter.21.cloned.1.call-update) | async-done | bytes 294928 | tf_op jit(solution)/shard_map/reduce_scatter | solution.py:310
  1224.6 72.0 %reduce-scatter.23.cloned.1.call-done = f32[96,768]{1,0:T(8,128)} async-done(((f32[768,768]{1,0:T(8,128)}), f32[96,768]{1,0:T(8,128)}) %reduce-scatter.23.cloned.1.call-update) | async-done | bytes 294928 | tf_op jit(solution)/shard_map/reduce_scatter | solution.py:311
  1296.5 65.3 %reduce-scatter.19.cloned.1.call-done = f32[96,192]{1,0:T(8,128)} async-done(((f32[768,192]{1,0:T(8,128)}), f32[96,192]{1,0:T(8,128)}) %reduce-scatter.19.cloned.1.call-update) | async-done | bytes 73744 | tf_op jit(solution)/shard_map/reduce_scatter | solution.py:309
  1361.9 72.4 %reduce-scatter.17.cloned.1.call-done = f32[96,3,192]{2,0,1:T(8,128)} async-done(((f32[768,3,192]{2,0,1:T(8,128)}), f32[96,3,192]{2,0,1:T(8,128)}) %reduce-scatter.17.cloned.1.call-update) | async-done | bytes 221200 | tf_op jit(solution)/shard_map/reduce_scatter | solution.py:308
  (562 shorter events, 391.6 us)
Async XLA Ops:
  8.0 80.5 %copy-start = (bf16[27,64]{1,0:T(8,128)(2,1)S(1)}, bf16[27,64]{1,0:T(8,128)(2,1)}, u32[]{:S(2)}) copy-start(bf16[27,64]{1,0:T(8,128)(2,1)} %param.28) | copy-start | bytes 10372
  8.1 80.9 %all-gather.7.cloned.1.call-start = ((), (), s32[]{:S(2)}) async-start(), calls=%async_computation.8 | async-start | bytes 7864320 | tf_op jit(solution)/shard_map/all_gather | solution.py:222
  14.4 41.0 %copy-start.48 = (bf16[96,192]{1,0:T(8,128)(2,1)S(1)}, bf16[96,192]{1,0:T(8,128)(2,1)}, u32[]{:S(2)}) copy-start(bf16[96,192]{1,0:T(8,128)(2,1)} %param.29) | copy-start | bytes 110596
  14.4 74.3 %copy-start.64 = (bf16[27,64]{1,0:T(8,128)(2,1)S(1)}, bf16[27,64]{1,0:T(8,128)(2,1)}, u32[]{:S(2)}) copy-start(bf16[27,64]{1,0:T(8,128)(2,1)} %param.27) | copy-start | bytes 10372
  14.5 342.4 %reduce-scatter.9.cloned.1.call-start = ((), (), s32[]{:S(2)}) async-start(), calls=%async_computation.9 | async-start | bytes 15728640 | tf_op jit(solution)/shard_map/reduce_scatter | solution.py:247
  54.6 72.4 %copy-start.28 = (bf16[768,3,192]{0,2,1:T(8,128)(2,1)}, bf16[768,3,192]{0,2,1:T(8,128)(2,1)S(1)}, u32[]{:S(2)}) copy-start(bf16[768,3,192]{0,2,1:T(8,128)(2,1)S(1)} %copy.163) | copy-start | bytes 2654212
  54.7 40.8 %copy-start.38 = (s32[14,14]{1,0:T(8,128)}, s32[14,14]{1,0:T(8,128)S(1)}, u32[]{:S(2)}) copy-start(s32[14,14]{1,0:T(8,128)S(1)} %subtract_add_fusion) | copy-start | bytes 2356
  226.2 8.9 copy-start.20
  226.2 8.9 copy-start.22
  226.2 8.9 copy-start.25
  258.2 98.7 %copy-start.15 = (bf16[1024,768]{1,0:T(8,128)(2,1)S(1)}, bf16[1024,768]{1,0:T(8,128)(2,1)}, u32[]{:S(2)}) copy-start(bf16[1024,768]{1,0:T(8,128)(2,1)} %param.22) | copy-start | bytes 4718596
  258.2 105.2 %all-gather.11.cloned.1.call-start = ((), (), s32[]{:S(2)}) async-start(), calls=%async_computation.11 | async-start | bytes 1327104 | tf_op jit(solution)/shard_map/all_gather | solution.py:211
  258.8 104.7 %all-gather.13.cloned.1.call-start = ((), (), s32[]{:S(2)}) async-start(), calls=%async_computation.12 | async-start | bytes 1327104 | tf_op jit(solution)/shard_map/all_gather | solution.py:212
  259.4 130.9 %all-gather.15.cloned.1.call-start = ((), (), s32[]{:S(2)}) async-start(), calls=%async_computation.14 | async-start | bytes 7864320 | tf_op jit(solution)/shard_map/all_gather | solution.py:262
  259.9 178.7 %all-gather.9.cloned.1.call-start = ((), (), s32[]{:S(2)}) async-start(), calls=%async_computation.10 | async-start | bytes 7864320 | tf_op jit(solution)/shard_map/all_gather | solution.py:255
  260.0 99.8 %copy-start.44 = (f32[768]{0:T(1024)}, f32[768]{0:T(1024)S(1)}, u32[]{:S(2)}) copy-start(f32[768]{0:T(1024)S(1)} %convert_element_type.146) | copy-start | bytes 9220
  363.3 286.4 %reduce-scatter.13.cloned.1.call-start = ((), (), s32[]{:S(2)}) async-start(), calls=%async_computation.15 | async-start | bytes 15728640 | tf_op jit(solution)/shard_map/reduce_scatter | solution.py:266
  540.4 10.1 copy-start.31
  550.6 159.9 %reduce-scatter.11.cloned.1.call-start = ((), (), s32[]{:S(2)}) async-start(), calls=%async_computation.13 | async-start | bytes 7864320 | tf_op jit(solution)/shard_map/reduce_scatter | solution.py:256
  590.5 59.1 %copy-start.13 = (f32[1024,768]{1,0:T(8,128)S(1)}, f32[1024,768]{1,0:T(8,128)}, u32[]{:S(2)}) copy-start(f32[1024,768]{1,0:T(8,128)} %copy-done.12) | copy-start | bytes 9437188
  590.5 59.1 %copy-start.37 = (f32[1024]{0:T(1024)S(1)}, f32[1024]{0:T(1024)}, u32[]{:S(2)}) copy-start(f32[1024]{0:T(1024)} %copy-done.36) | copy-start | bytes 12292
  590.5 59.1 %copy-start.45 = (f32[768]{0:T(1024)S(1)}, f32[768]{0:T(1024)}, u32[]{:S(2)}) copy-start(f32[768]{0:T(1024)} %copy-done.44) | copy-start | bytes 9220
  590.5 59.1 %copy-start.47 = (f32[1024]{0:T(1024)S(1)}, f32[1024]{0:T(1024)}, u32[]{:S(2)}) copy-start(f32[1024]{0:T(1024)} %copy-done.46) | copy-start | bytes 12292
  590.6 172.5 %all-gather.17.cloned.1.call-start = ((), (), s32[]{:S(2)}) async-start(), calls=%async_computation.16 | async-start | bytes 7864320 | tf_op jit(solution)/shard_map/all_gather | solution.py:278
  716.5 434.4 %reduce-scatter.15.cloned.1.call-start = ((), (), s32[]{:S(2)}) async-start(), calls=%async_computation.17 | async-start | bytes 7864320 | tf_op jit(solution)/shard_map/reduce_scatter | solution.py:295
  783.1 8.5 copy-start.21
  783.1 8.5 copy-start.23
  783.1 8.5 copy-start.26
  783.2 8.5 copy-start.30
  793.3 8.1 copy-start.9
  838.1 8.1 copy-start.9
  927.5 8.1 copy-start.9
  972.2 8.1 copy-start.9
  1092.4 132.1 %reduce-scatter.21.cloned.1.call-start = ((), (), s32[]{:S(2)}) async-start(), calls=%async_computation.20 | async-start | bytes 2654208 | tf_op jit(solution)/shard_map/reduce_scatter | solution.py:310
  1093.0 203.5 %reduce-scatter.23.cloned.1.call-start = ((), (), s32[]{:S(2)}) async-start(), calls=%async_computation.21 | async-start | bytes 2654208 | tf_op jit(solution)/shard_map/reduce_scatter | solution.py:311
  1093.6 268.3 %reduce-scatter.19.cloned.1.call-start = ((), (), s32[]{:S(2)}) async-start(), calls=%async_computation.19 | async-start | bytes 884736 | tf_op jit(solution)/shard_map/reduce_scatter | solution.py:309
  1108.0 326.2 %reduce-scatter.17.cloned.1.call-start = ((), (), s32[]{:S(2)}) async-start(), calls=%async_computation.18 | async-start | bytes 2654208 | tf_op jit(solution)/shard_map/reduce_scatter | solution.py:308
  1117.8 27.2 %copy-start.39 = (s32[14,14]{1,0:T(8,128)S(1)}, s32[14,14]{1,0:T(8,128)}, u32[]{:S(2)}) copy-start(s32[14,14]{1,0:T(8,128)} %copy-done.38) | copy-start | bytes 2356
  1117.8 33.1 %copy-start.16 = (bf16[1024,768]{1,0:T(8,128)(2,1)S(1)}, bf16[1024,768]{1,0:T(8,128)(2,1)}, u32[]{:S(2)}) copy-start(bf16[1024,768]{1,0:T(8,128)(2,1)} %param.22) | copy-start | bytes 4718596
  1117.8 33.1 %copy-start.35 = (f32[1024]{0:T(1024)S(1)}, f32[1024]{0:T(1024)}, u32[]{:S(2)}) copy-start(f32[1024]{0:T(1024)} %copy-done.34) | copy-start | bytes 12292
  1117.8 33.1 %copy-start.41 = (f32[1024]{0:T(1024)S(1)}, f32[1024]{0:T(1024)}, u32[]{:S(2)}) copy-start(f32[1024]{0:T(1024)} %copy-done.40) | copy-start | bytes 12292
  1117.8 33.1 %copy-start.43 = (f32[768]{0:T(1024)S(1)}, f32[768]{0:T(1024)}, u32[]{:S(2)}) copy-start(f32[768]{0:T(1024)} %copy-done.42) | copy-start | bytes 9220
  1122.4 31.7 %copy-start.49 = (f32[768]{0:T(1024)S(1)}, f32[768]{0:T(1024)}, u32[]{:S(2)}) copy-start(f32[768]{0:T(1024)} %get-tuple-element.318) | copy-start | bytes 9220
  1122.4 31.7 %copy-start.50 = (f32[768]{0:T(1024)S(1)}, f32[768]{0:T(1024)}, u32[]{:S(2)}) copy-start(f32[768]{0:T(1024)} %get-tuple-element.323) | copy-start | bytes 9220
  1122.4 31.7 %copy-start.51 = (f32[768]{0:T(1024)S(1)}, f32[768]{0:T(1024)}, u32[]{:S(2)}) copy-start(f32[768]{0:T(1024)} %get-tuple-element.394) | copy-start | bytes 9220
  1122.4 31.7 %copy-start.52 = (f32[768]{0:T(1024)S(1)}, f32[768]{0:T(1024)}, u32[]{:S(2)}) copy-start(f32[768]{0:T(1024)} %get-tuple-element.408) | copy-start | bytes 9220
  1150.9 44.8 %copy-start.24 = (bf16[1024,768]{1,0:T(8,128)(2,1)S(1)}, bf16[1024,768]{1,0:T(8,128)(2,1)}, u32[]{:S(2)}) copy-start(bf16[1024,768]{1,0:T(8,128)(2,1)} %reduce-scatter.15.cloned.1.call-done) | copy-start | bytes 4718596
  1195.7 238.5 %copy-start.1 = (bf16[27,64]{1,0:T(8,128)(2,1)S(1)}, bf16[27,64]{1,0:T(8,128)(2,1)}, u32[]{:S(2)}) copy-start(bf16[27,64]{1,0:T(8,128)(2,1)} %param.28) | copy-start | bytes 10372
  (82 other events, 235.9 us)
Sparse Core Ops, SparseCore 0:
  14.6 49.0 all-gather.6
  258.3 98.4 reduce-scatter.8
  716.7 46.3 all-gather.16
  1092.5 58.3 reduce-scatter.14
  1154.8 69.6 reduce-scatter.20
  1228.5 68.0 reduce-scatter.22
  1300.4 61.4 reduce-scatter.18
  1366.3 67.8 reduce-scatter.16
Sparse Core Ops, SparseCore 1:
  260.9 40.6 all-gather.10
  303.6 39.8 all-gather.12
  344.9 45.3 all-gather.14
  392.4 46.2 all-gather.8
  550.7 98.9 reduce-scatter.12
  652.2 58.2 reduce-scatter.10
where the time goes:
time: 1460 us; the launch traced here: 1440 us
  waiting for transfers between devices  577 us (40%)
  local copies, waits for them, and re-layouts  329 us (23%)
  matrix products  328 us (22%)
  blocking collectives  136 us (9%)
  other arithmetic  53.1 us (4%)
  between operations  16.8 us (1%)
    reduce_scatter x1, waiting for transfers between devices, body(): lax.psum_scatter(contract_last(on_grid, output_full), 'tensor', scatter_d...  96.8 us
    dot_general x10, matrix products, contract_first(): lax.dot_general(left, right, (((0,), (0,)), ((), ())), preferred_element_...  78 us
    reduce_scatter x1, waiting for transfers between devices, body(): lax.psum_scatter(grad_qkv_weight, 'dp', scatter_dimension=0, tiled=True)  72.4 us
    reduce_scatter x1, waiting for transfers between devices, body(): lax.psum_scatter(grad_down, 'dp', scatter_dimension=0, tiled=True)  72 us
    reduce_scatter x1, waiting for transfers between devices, body(): lax.psum_scatter(grad_output, 'dp', scatter_dimension=0, tiled=True)  65.3 us
    dot_general x4, matrix products, contract_last(): lax.dot_general(left, right, (((1,), (1,)), ((), ())), preferred_element_...  61.7 us
    reduce_scatter x1, waiting for transfers between devices, body(): lax.psum_scatter(contract_last(deltas, up_full), 'tensor', scatter_dimens...  58.4 us
    reduce_scatter x1, waiting for transfers between devices, body(): lax.psum_scatter(feed_rows(normed_two_all, up_full, up_shift, down_full)....  57.1 us
  transfers between devices with their start and end apart: 14, of which 11 were waited for; matrix products, arithmetic and copies ran while one was open for 6% of the time, Pallas kernels for 0%

commit v1 on v0

--- a/solution.py
+++ b/solution.py
@@ -252,7 +252,14 @@
     hat_two, inverse_two = norm_parts(hidden_one)
     normed_two = (hat_two * gain_two + second_shift.astype(jnp.float32)).astype(jnp.bfloat16)
     up_shift = up_bias.astype(jnp.float32)
-    normed_two_all = lax.all_gather(normed_two, "tensor", axis=0, tiled=True)
+    ring = [normed_two]
+    for hop in range(3):
+        ring.append(lax.ppermute(ring[-1], "tensor", [(dev, (dev + 1) % 4) for dev in range(4)]))
+    normed_two_all = jnp.roll(
+        jnp.concatenate(ring[::-1], axis=0),
+        (lax.axis_index("tensor") + 1) * ring[0].shape[0],
+        axis=0,
+    )
     feed = lax.psum_scatter(
         feed_rows(normed_two_all, up_full, up_shift, down_full).astype(jnp.bfloat16),
         "tensor",

time: 1460 us -> 1470 us (level)
    ppermute x0 -> x3, waiting for transfers between devices: none -> 84.5 us  [body(): lax.ppermute(ring[-1], 'tensor', [(dev, (dev + 1) % 4) for dev in range(4)])]
    all_gather x1 -> x0, waiting for transfers between devices: 48.4 us -> none  [body(): normed_two_all = lax.all_gather(normed_two, 'tensor', axis=0, tiled=True)]
    all_gather x1, waiting for transfers between devices: 26.8 us -> 0.01 us  [body(): grads_all = lax.all_gather(cotangent, 'tensor', axis=0, tiled=True)]
  transfers between devices with their start and end apart: 14 -> 16, of which waited for: 11 -> 12; matrix products, arithmetic and copies ran while one was open for 6% -> 6% of each run, Pallas kernels for 0% -> 0%
where the time goes in v1:
time: 1470 us; the launch traced here: 1460 us
  waiting for transfers between devices  587 us (40%)
  local copies, waits for them, and re-layouts  337 us (23%)
  matrix products  327 us (22%)
  blocking collectives  136 us (9%)
  other arithmetic  53.5 us (4%)
  between operations  16.9 us (1%)
    reduce_scatter x1, waiting for transfers between devices, body(): lax.psum_scatter(contract_last(on_grid, output_full), 'tensor', scatter_d...  96.7 us
    ppermute x3, waiting for transfers between devices, body(): lax.ppermute(ring[-1], 'tensor', [(dev, (dev + 1) % 4) for dev in range(4)])  84.5 us
    dot_general x10, matrix products, contract_first(): lax.dot_general(left, right, (((0,), (0,)), ((), ())), preferred_element_...  78.2 us
    reduce_scatter x1, waiting for transfers between devices, body(): lax.psum_scatter(grad_qkv_weight, 'dp', scatter_dimension=0, tiled=True)  72.4 us
    reduce_scatter x1, waiting for transfers between devices, body(): lax.psum_scatter(grad_down, 'dp', scatter_dimension=0, tiled=True)  72 us
    reduce_scatter x1, waiting for transfers between devices, body(): lax.psum_scatter(grad_output, 'dp', scatter_dimension=0, tiled=True)  65.4 us
    dot_general x4, matrix products, contract_last(): lax.dot_general(left, right, (((1,), (1,)), ((), ())), preferred_element_...  61.3 us
    reduce_scatter x1, waiting for transfers between devices, body(): lax.psum_scatter(contract_last(deltas, up_full), 'tensor', scatter_dimens...  59 us
  transfers between devices with their start and end apart: 16, of which 12 were waited for; matrix products, arithmetic and copies ran while one was open for 6% of the time, Pallas kernels for 0%

profile of v1, /device:TPU:0, one launch (start us, length us, event | category | flops | bytes accessed | tf_op | source)
XLA Modules:
  0.0 1461.3 jit_solution(17425841195687642743)
XLA Ops:
  14.9 38.8 %all_gather.22 = bf16[768,3,192]{2,1,0:T(4,128)(2,1)S(1)} all-gather(bf16[96,3,192]{2,1,0:T(4,128)(2,1)S(1)} %copy.162), channel_id=1, replica_groups=mesh['dp'=8,'tensor'=4] {'dp'}, dimensions={0}, use_global_device_ids=true | all-gather | bytes 995328 | tf_op jit(solution)/shard_map/all_gather | solution.py:209
  55.4 33.1 %all_gather.23 = bf16[768,192]{1,0:T(8,128)(2,1)} all-gather(bf16[96,192]{1,0:T(8,128)(2,1)S(1)} %copy-done.49), channel_id=1, replica_groups=mesh['dp'=8,'tensor'=4] {'dp'}, dimensions={0}, use_global_device_ids=true | all-gather | bytes 331776 | tf_op jit(solution)/shard_map/all_gather | solution.py:210
  89.0 6.5 pad.8
  95.5 11.5 reshape.269
  107.0 7.8 copy.161
  114.7 12.2 reshape_reshape.12
  126.9 9.8 add_convert_fusion
  136.7 17.7 %reshape.271 = bf16[5,5,196,3,3,64]{2,1,0,5,4,3:T(8,128)(2,1)} reshape(bf16[4900,576]{0,1:T(8,128)(2,1)} %add_convert_fusion) | data formatting | bytes 11289600 | tf_op jit(solution)/shard_map/reshape | solution.py:234
  154.4 9.7 copy.164
  164.1 62.1 %while.44 = (s32[]{:T(128)}, bf16[5,5,196,3,64]{2,4,3,1,0:T(8,128)(2,1)}, f32[5,5,3,196,1]{3,2,1,4,0:T(4,128)}, bf16[5,5,196,3,3,64]{2,5,4,1,3,0:T(8,128)(2,1)},...) while((s32[]{:T(128)}, ...), condition=%wide.region_5.6_spmd, body=%wide.region_2.5_spmd.sunk | while | flops 355972256 | bytes 23991828 | solution.py:245
  226.2 8.9 copy.165
  235.1 9.3 reshape_reshape.13
  251.9 6.3 fusion.247
  260.1 96.7 %reduce-scatter.9.cloned.1.call-done = f32[1024,768]{1,0:T(8,128)} async-done(((f32[4096,768]{1,0:T(8,128)}), f32[1024,768]{1,0:T(8,128)}) %reduce-scatter.9.cloned.1.call-update) | async-done | bytes 3145744 | tf_op jit(solution)/shard_map/reduce_scatter | solution.py:247
  360.9 44.6 %collective-permute-done = bf16[1024,768]{1,0:T(8,128)(2,1)S(1)} collective-permute-done((bf16[1024,768]{1,0:T(8,128)(2,1)S(1)}, bf16[1024,768]{1,0:T(8,128)(2,1)S(1)}, u32[]{:S(2)}, u32[]{:S(2)}) %collective-permute-start) | collective-permute-done | bytes 1572896 | tf_op jit(solution)/shard_map/ppermute | solution.py:257
  406.6 19.9 %collective-permute-done.1 = bf16[1024,768]{1,0:T(8,128)(2,1)} collective-permute-done((bf16[1024,768]{1,0:T(8,128)(2,1)S(1)}, bf16[1024,768]{1,0:T(8,128)(2,1)}, u32[]{:S(2)}, u32[]{:S(2)}) %collective-permute-start.1) | collective-permute-done | bytes 1572896 | tf_op jit(solution)/shard_map/ppermute | solution.py:257
  427.0 20.0 %collective-permute-done.2 = bf16[1024,768]{1,0:T(8,128)(2,1)} collective-permute-done((bf16[1024,768]{1,0:T(8,128)(2,1)}, bf16[1024,768]{1,0:T(8,128)(2,1)}, u32[]{:S(2)}, u32[]{:S(2)}) %collective-permute-start.2) | collective-permute-done | bytes 1572896 | tf_op jit(solution)/shard_map/ppermute | solution.py:257
  457.5 101.7 %while.45 = (s32[]{:T(128)}, f32[768,768]{1,0:T(8,128)}, f32[768,768]{1,0:T(8,128)}, f32[768]{0:T(1024)S(1)}, bf16[4,1024,768]{2,1,0:T(8,128)(2,1)}, /*index=5*/...) while((s32[]{:T(128)}, f32[768,768]{1,0:T(8,128)}, ...), condition=%wide.region_12.13_spmd.clone, body=%wide.region_10.12_spmd.clone.sunk | while | flops 4896326144 | bytes 63722192 | solution.py:184
  460.8 5.3 convert_reduce_fusion.7
  471.9 10.3 select_add_fusion.7
  485.5 5.3 convert_reduce_fusion.7
  497.4 10.6 select_add_fusion.7
  511.2 5.3 convert_reduce_fusion.7
  523.0 10.6 select_add_fusion.7
  536.9 5.3 convert_reduce_fusion.7
  548.7 10.6 select_add_fusion.7
  559.3 10.2 fusion.248
  571.1 37.8 %convolution_convert_fusion.1 = bf16[4096,768]{1,0:T(8,128)(2,1)} fusion(bf16[768,768]{1,0:T(8,128)(2,1)S(1)} %copy-done.64, f32[768]{0:T(1024)S(1)} %get-tuple-element.758, bf16[4096,768]{1,0:T(8,128)(2,1)} %bitcast.319, bf16[768,768]{1,0:T(8,128)(2,1)S(1)} %copy-done.62), kind=kOutput, calls=%fused_computation.213 | convolution fusion | flops 9874440192 | bytes 14945280 | tf_op jit(solution)/shard_map/dot_general | solution.py:75
  609.6 59.0 %reduce-scatter.13.cloned.1.call-done = f32[1024,768]{1,0:T(8,128)} async-done(((f32[4096,768]{1,0:T(8,128)}), f32[1024,768]{1,0:T(8,128)}) %reduce-scatter.13.cloned.1.call-update) | async-done | bytes 3145744 | tf_op jit(solution)/shard_map/reduce_scatter | solution.py:273
  672.3 57.1 %reduce-scatter.11.cloned.1.call-done = bf16[1024,768]{1,0:T(8,128)(2,1)} async-done(((bf16[4096,768]{1,0:T(8,128)(2,1)}), bf16[1024,768]{1,0:T(8,128)(2,1)}) %reduce-scatter.11.cloned.1.call-update) | async-done | bytes 1572880 | tf_op jit(solution)/shard_map/reduce_scatter | solution.py:263
  729.4 6.1 convert_reduce_fusion.5
  735.6 46.5 %all-gather.14.cloned.1.call-done = bf16[4096,768]{1,0:T(8,128)(2,1)} async-done(((bf16[1024,768]{1,0:T(8,128)(2,1)}), bf16[4096,768]{1,0:T(8,128)(2,1)}) %all-gather.14.cloned.1.call-update) | async-done | bytes 6291472 | tf_op jit(solution)/shard_map/all_gather | solution.py:285
  802.1 8.5 copy.170
  810.6 224.2 %while.46 = (s32[]{:T(128)}, f32[14,14,64]{2,1,0:T(8,128)S(1)}, f32[14,14,64]{2,1,0:T(8,128)S(1)}, bf16[5,5,196,3,3,64]{2,5,4,1,3,0:T(8,128)(2,1)}, bf16[5,5,196...) while((s32[]{:T(128)}, f32[14,14,64]{2,1,0:T(8,128)S(1)}, ...), condition=%wide.region_18.19_spmd.clone, body=%wide.region_16.18_spmd.clone.sunk | while | flops 741679872 | bytes 70086392 | solution.py:294
  1034.8 20.7 %copy.171 = bf16[5,5,196,3,3,64]{5,4,3,2,1,0:T(4,128)(2,1)} copy(bf16[5,5,196,3,3,64]{2,5,4,1,3,0:T(8,128)(2,1)} %get-tuple-element.171) | data formatting | bytes 11289600 | tf_op jit(solution)/shard_map/while | solution.py:294
  1055.5 26.6 %reshape_reshape.15 = bf16[1,5,5,14,14,576]{5,4,3,2,1,0:T(8,128)(2,1)} reshape(bf16[5,5,196,3,3,64]{5,4,3,2,1,0:T(4,128)(2,1)} %copy.171) | data formatting | bytes 11289600 | tf_op jit(solution)/shard_map/reshape;reshape | solution.py:50
  1082.1 6.5 copy.172
  1088.6 10.7 reshape.279
  1104.6 6.9 convolution_convert_fusion
  1112.8 8.0 copy.173
  1120.8 6.4 fusion.249
  1127.3 9.7 fusion.182
  1141.8 22.4 %all-reduce.3 = (f32[2,192]{1,0:T(2,128)}, f32[768]{0:T(1024)}) all-reduce(f32[2,192]{1,0:T(2,128)S(1)} %pad_maximum_fusion.3, f32[768]{0:T(1024)S(1)} %copy-done.35), channel_id=1, replica_groups=mesh['dp'=8,'tensor'=4] {'dp'}, use_global_device_ids=true, to_apply=%region_28.29 | all-reduce | flops 1152 | bytes 9216 | tf_op jit(solution)/shard_map/psum | solution.py:342
  1173.2 41.7 %all-reduce.2 = (f32[768]{0:T(1024)}, f32[768]{0:T(1024)}, f32[27,64]{1,0:T(8,128)}, f32[27,64]{1,0:T(8,128)}, f32[768]{0:T(1024)}, /*index=5*/f32[768]{0:T(1024)}, f32[768]{0:T(1024)}, f32[768]{0:T(1024)}) all-reduce(f32[768]{0:T(1024)S(1)} %get-tuple-element.320, ...), channel_id=1, replica_groups=mesh['dp'=8,'tensor'=4] {'dp','tensor'}, use_global_device_ids=true, to_apply=%region_23.24 | all-reduce | flops 8064 | bytes 64512 | tf_op jit(solution)/shard_map/psum | solution.py:329
  1218.6 25.1 %reduce-scatter.21.cloned.1.call-done = f32[96,768]{1,0:T(8,128)} async-done(((f32[768,768]{1,0:T(8,128)}), f32[96,768]{1,0:T(8,128)}) %reduce-scatter.21.cloned.1.call-update) | async-done | bytes 294928 | tf_op jit(solution)/shard_map/reduce_scatter | solution.py:317
  1243.8 72.0 %reduce-scatter.23.cloned.1.call-done = f32[96,768]{1,0:T(8,128)} async-done(((f32[768,768]{1,0:T(8,128)}), f32[96,768]{1,0:T(8,128)}) %reduce-scatter.23.cloned.1.call-update) | async-done | bytes 294928 | tf_op jit(solution)/shard_map/reduce_scatter | solution.py:318
  1315.8 65.4 %reduce-scatter.19.cloned.1.call-done = f32[96,192]{1,0:T(8,128)} async-done(((f32[768,192]{1,0:T(8,128)}), f32[96,192]{1,0:T(8,128)}) %reduce-scatter.19.cloned.1.call-update) | async-done | bytes 73744 | tf_op jit(solution)/shard_map/reduce_scatter | solution.py:316
  1381.1 72.4 %reduce-scatter.17.cloned.1.call-done = f32[96,3,192]{2,0,1:T(8,128)} async-done(((f32[768,3,192]{2,0,1:T(8,128)}), f32[96,3,192]{2,0,1:T(8,128)}) %reduce-scatter.17.cloned.1.call-update) | async-done | bytes 221200 | tf_op jit(solution)/shard_map/reduce_scatter | solution.py:315
  (576 shorter events, 406.4 us)
Async XLA Ops:
  8.0 80.5 %copy-start = (bf16[27,64]{1,0:T(8,128)(2,1)S(1)}, bf16[27,64]{1,0:T(8,128)(2,1)}, u32[]{:S(2)}) copy-start(bf16[27,64]{1,0:T(8,128)(2,1)} %param.28) | copy-start | bytes 10372
  8.1 80.9 %all-gather.6.cloned.1.call-start = ((), (), s32[]{:S(2)}) async-start(), calls=%async_computation.8 | async-start | bytes 7864320 | tf_op jit(solution)/shard_map/all_gather | solution.py:222
  14.4 41.0 %copy-start.49 = (bf16[96,192]{1,0:T(8,128)(2,1)S(1)}, bf16[96,192]{1,0:T(8,128)(2,1)}, u32[]{:S(2)}) copy-start(bf16[96,192]{1,0:T(8,128)(2,1)} %param.29) | copy-start | bytes 110596
  14.4 74.3 %copy-start.65 = (bf16[27,64]{1,0:T(8,128)(2,1)S(1)}, bf16[27,64]{1,0:T(8,128)(2,1)}, u32[]{:S(2)}) copy-start(bf16[27,64]{1,0:T(8,128)(2,1)} %param.27) | copy-start | bytes 10372
  14.4 342.4 %reduce-scatter.9.cloned.1.call-start = ((), (), s32[]{:S(2)}) async-start(), calls=%async_computation.9 | async-start | bytes 15728640 | tf_op jit(solution)/shard_map/reduce_scatter | solution.py:247
  54.6 72.3 %copy-start.29 = (bf16[768,3,192]{0,2,1:T(8,128)(2,1)}, bf16[768,3,192]{0,2,1:T(8,128)(2,1)S(1)}, u32[]{:S(2)}) copy-start(bf16[768,3,192]{0,2,1:T(8,128)(2,1)S(1)} %copy.163) | copy-start | bytes 2654212
  54.7 40.8 %copy-start.43 = (s32[14,14]{1,0:T(8,128)}, s32[14,14]{1,0:T(8,128)S(1)}, u32[]{:S(2)}) copy-start(s32[14,14]{1,0:T(8,128)S(1)} %subtract_add_fusion) | copy-start | bytes 2356
  226.2 8.9 copy-start.19
  226.2 8.9 copy-start.21
  226.2 8.9 copy-start.26
  258.2 199.3 %all-gather.8.cloned.1.call-start = ((), (), s32[]{:S(2)}) async-start(), calls=%async_computation.10 | async-start | bytes 1327104 | tf_op jit(solution)/shard_map/all_gather | solution.py:211
  258.8 198.7 %all-gather.10.cloned.1.call-start = ((), (), s32[]{:S(2)}) async-start(), calls=%async_computation.11 | async-start | bytes 1327104 | tf_op jit(solution)/shard_map/all_gather | solution.py:212
  259.4 198.2 %all-gather.12.cloned.1.call-start = ((), (), s32[]{:S(2)}) async-start(), calls=%async_computation.13 | async-start | bytes 7864320 | tf_op jit(solution)/shard_map/all_gather | solution.py:269
  259.9 408.6 %reduce-scatter.13.cloned.1.call-start = ((), (), s32[]{:S(2)}) async-start(), calls=%async_computation.14 | async-start | bytes 15728640 | tf_op jit(solution)/shard_map/reduce_scatter | solution.py:273
  260.0 193.9 %copy-start.37 = (f32[768]{0:T(1024)}, f32[768]{0:T(1024)S(1)}, u32[]{:S(2)}) copy-start(f32[768]{0:T(1024)S(1)} %convert_element_type.146) | copy-start | bytes 9220
  359.6 94.3 %copy-start.10 = (f32[1024,768]{1,0:T(8,128)}, f32[1024,768]{1,0:T(8,128)S(1)}, u32[]{:S(2)}) copy-start(f32[1024,768]{1,0:T(8,128)S(1)} %get-tuple-element.398) | copy-start | bytes 9437188
  359.7 94.3 %copy-start.32 = (f32[1024]{0:T(1024)}, f32[1024]{0:T(1024)S(1)}, u32[]{:S(2)}) copy-start(f32[1024]{0:T(1024)S(1)} %broadcast_multiply_fusion.4) | copy-start | bytes 12292
  360.2 66.8 %copy-start.60 = (bf16[768]{0:T(1024)(128)(2,1)S(1)}, bf16[768]{0:T(1024)(128)(2,1)}, u32[]{:S(2)}) copy-start(bf16[768]{0:T(1024)(128)(2,1)} %param.34) | copy-start | bytes 4612
  360.2 93.7 %copy-start.39 = (f32[1024]{0:T(1024)}, f32[1024]{0:T(1024)S(1)}, u32[]{:S(2)}) copy-start(f32[1024]{0:T(1024)S(1)} %add_rsqrt_fusion) | copy-start | bytes 12292
  360.8 44.6 %collective-permute-start = (bf16[1024,768]{1,0:T(8,128)(2,1)S(1)}, bf16[1024,768]{1,0:T(8,128)(2,1)S(1)}, u32[]{:S(2)}, u32[]{:S(2)}) collective-permute-start(bf16[1024,768]{1,0:T(8,128)(2,1)S(1)} %add_convert_fusion.2), channel_id=1, source_target_pairs={{0,1},{1,2},{2,3},{3,0},{4,5},{5,6},{6,7},{7,4},{8,9},{9,10},{10,1... | collective-permute-start | bytes 4718600 | tf_op jit(solution)/shard_map/ppermute | solution.py:257
  406.6 19.9 %collective-permute-start.1 = (bf16[1024,768]{1,0:T(8,128)(2,1)S(1)}, bf16[1024,768]{1,0:T(8,128)(2,1)}, u32[]{:S(2)}, u32[]{:S(2)}) collective-permute-start(bf16[1024,768]{1,0:T(8,128)(2,1)S(1)} %collective-permute-done), channel_id=1, source_target_pairs={{0,1},{1,2},{2,3},{3,0},{4,5},{5,6},{6,7},{7,4},{8,9},{9,10},{10,1... | collective-permute-start | bytes 4718600 | tf_op jit(solution)/shard_map/ppermute | solution.py:257
  426.5 20.5 %collective-permute-start.2 = (bf16[1024,768]{1,0:T(8,128)(2,1)}, bf16[1024,768]{1,0:T(8,128)(2,1)}, u32[]{:S(2)}, u32[]{:S(2)}) collective-permute-start(bf16[1024,768]{1,0:T(8,128)(2,1)} %collective-permute-done.1), channel_id=1, source_target_pairs={{0,1},{1,2},{2,3},{3,0},{4,5},{5,6},{6,7},{7,4},{8,9},{9,10},{10,1... | collective-permute-start | bytes 4718600 | tf_op jit(solution)/shard_map/ppermute | solution.py:257
  427.0 23.1 %copy-start.25 = (bf16[1024,768]{1,0:T(8,128)(2,1)S(1)}, bf16[1024,768]{1,0:T(8,128)(2,1)}, u32[]{:S(2)}) copy-start(bf16[1024,768]{1,0:T(8,128)(2,1)} %copy-done.24) | copy-start | bytes 4718596
  559.3 10.2 copy-start.34
  569.5 159.9 %reduce-scatter.11.cloned.1.call-start = ((), (), s32[]{:S(2)}) async-start(), calls=%async_computation.12 | async-start | bytes 7864320 | tf_op jit(solution)/shard_map/reduce_scatter | solution.py:263
  608.9 59.6 %copy-start.11 = (f32[1024,768]{1,0:T(8,128)S(1)}, f32[1024,768]{1,0:T(8,128)}, u32[]{:S(2)}) copy-start(f32[1024,768]{1,0:T(8,128)} %copy-done.10) | copy-start | bytes 9437188
  608.9 59.6 %copy-start.33 = (f32[1024]{0:T(1024)S(1)}, f32[1024]{0:T(1024)}, u32[]{:S(2)}) copy-start(f32[1024]{0:T(1024)} %copy-done.32) | copy-start | bytes 12292
  608.9 59.6 %copy-start.38 = (f32[768]{0:T(1024)S(1)}, f32[768]{0:T(1024)}, u32[]{:S(2)}) copy-start(f32[768]{0:T(1024)} %copy-done.37) | copy-start | bytes 9220
  608.9 59.6 %copy-start.40 = (f32[1024]{0:T(1024)S(1)}, f32[1024]{0:T(1024)}, u32[]{:S(2)}) copy-start(f32[1024]{0:T(1024)} %copy-done.39) | copy-start | bytes 12292
  609.0 173.0 %all-gather.14.cloned.1.call-start = ((), (), s32[]{:S(2)}) async-start(), calls=%async_computation.15 | async-start | bytes 7864320 | tf_op jit(solution)/shard_map/all_gather | solution.py:285
  735.5 434.7 %reduce-scatter.15.cloned.1.call-start = ((), (), s32[]{:S(2)}) async-start(), calls=%async_computation.16 | async-start | bytes 7864320 | tf_op jit(solution)/shard_map/reduce_scatter | solution.py:302
  802.1 8.5 copy-start.27
  802.1 8.5 copy-start.31
  1111.6 132.1 %reduce-scatter.21.cloned.1.call-start = ((), (), s32[]{:S(2)}) async-start(), calls=%async_computation.19 | async-start | bytes 2654208 | tf_op jit(solution)/shard_map/reduce_scatter | solution.py:317
  1112.2 203.6 %reduce-scatter.23.cloned.1.call-start = ((), (), s32[]{:S(2)}) async-start(), calls=%async_computation.20 | async-start | bytes 2654208 | tf_op jit(solution)/shard_map/reduce_scatter | solution.py:318
  1112.8 268.4 %reduce-scatter.19.cloned.1.call-start = ((), (), s32[]{:S(2)}) async-start(), calls=%async_computation.18 | async-start | bytes 884736 | tf_op jit(solution)/shard_map/reduce_scatter | solution.py:316
  1127.2 326.3 %reduce-scatter.17.cloned.1.call-start = ((), (), s32[]{:S(2)}) async-start(), calls=%async_computation.17 | async-start | bytes 2654208 | tf_op jit(solution)/shard_map/reduce_scatter | solution.py:315
  1137.0 27.2 %copy-start.44 = (s32[14,14]{1,0:T(8,128)S(1)}, s32[14,14]{1,0:T(8,128)}, u32[]{:S(2)}) copy-start(s32[14,14]{1,0:T(8,128)} %copy-done.43) | copy-start | bytes 2356
  1137.0 33.1 %copy-start.15 = (bf16[1024,768]{1,0:T(8,128)(2,1)S(1)}, bf16[1024,768]{1,0:T(8,128)(2,1)}, u32[]{:S(2)}) copy-start(bf16[1024,768]{1,0:T(8,128)(2,1)} %param.22) | copy-start | bytes 4718596
  1137.0 33.1 %copy-start.42 = (f32[1024]{0:T(1024)S(1)}, f32[1024]{0:T(1024)}, u32[]{:S(2)}) copy-start(f32[1024]{0:T(1024)} %copy-done.41) | copy-start | bytes 12292
  1137.0 33.1 %copy-start.46 = (f32[1024]{0:T(1024)S(1)}, f32[1024]{0:T(1024)}, u32[]{:S(2)}) copy-start(f32[1024]{0:T(1024)} %copy-done.45) | copy-start | bytes 12292
  1137.0 33.1 %copy-start.48 = (f32[768]{0:T(1024)S(1)}, f32[768]{0:T(1024)}, u32[]{:S(2)}) copy-start(f32[768]{0:T(1024)} %copy-done.47) | copy-start | bytes 9220
  1141.5 31.7 %copy-start.50 = (f32[768]{0:T(1024)S(1)}, f32[768]{0:T(1024)}, u32[]{:S(2)}) copy-start(f32[768]{0:T(1024)} %get-tuple-element.318) | copy-start | bytes 9220
  1141.5 31.7 %copy-start.51 = (f32[768]{0:T(1024)S(1)}, f32[768]{0:T(1024)}, u32[]{:S(2)}) copy-start(f32[768]{0:T(1024)} %get-tuple-element.323) | copy-start | bytes 9220
  1141.5 31.7 %copy-start.52 = (f32[768]{0:T(1024)S(1)}, f32[768]{0:T(1024)}, u32[]{:S(2)}) copy-start(f32[768]{0:T(1024)} %get-tuple-element.394) | copy-start | bytes 9220
  1141.6 31.7 %copy-start.53 = (f32[768]{0:T(1024)S(1)}, f32[768]{0:T(1024)}, u32[]{:S(2)}) copy-start(f32[768]{0:T(1024)} %get-tuple-element.408) | copy-start | bytes 9220
  1170.1 44.8 %copy-start.23 = (bf16[1024,768]{1,0:T(8,128)(2,1)S(1)}, bf16[1024,768]{1,0:T(8,128)(2,1)}, u32[]{:S(2)}) copy-start(bf16[1024,768]{1,0:T(8,128)(2,1)} %reduce-scatter.15.cloned.1.call-done) | copy-start | bytes 4718596
  1215.0 238.6 %copy-start.1 = (bf16[27,64]{1,0:T(8,128)(2,1)S(1)}, bf16[27,64]{1,0:T(8,128)(2,1)}, u32[]{:S(2)}) copy-start(bf16[27,64]{1,0:T(8,128)(2,1)} %param.28) | copy-start | bytes 10372
  (85 other events, 278.2 us)
Sparse Core Ops, SparseCore 0:
  14.6 49.0 all-gather.5
  258.3 98.4 reduce-scatter.8
  735.6 46.3 all-gather.13
  1111.7 58.3 reduce-scatter.14
  1174.0 69.6 reduce-scatter.20
  1247.7 68.0 reduce-scatter.22
  1319.7 61.4 reduce-scatter.18
  1385.6 67.8 reduce-scatter.16
Sparse Core Ops, SparseCore 1:
  260.8 40.6 all-gather.7
  303.6 40.0 all-gather.9
  345.1 57.5 all-gather.11
  569.6 98.9 reduce-scatter.12
  671.1 58.2 reduce-scatter.10
